TPU v7x, 32 devices: a whole 2x2x4 slice. The times are simulated.
32 devices in a mesh: team: 8 (over z, core), member: 4 (over y, x).
Axes of the slice: x: 2, y: 2, z: 4, core: 2. Of those that a mesh axis runs over, the one named last changes fastest.
Arguments:
- state_start: float32 [24, 512, 512], P(None, 'team', 'member'), may hold values from -6 to 6
- state_section: float32 [24, 512, 512], P(None, 'team', 'member'), may hold values from -6 to 6
- velocity: float32 [2, 512, 512], P(None, 'team', 'member'), may hold values from -3 to 3
- diffusivity: float32 [24], replicated, may hold values from 0.05 to 0.5
- flame_cells: int32 [32, 128], P(('team', 'member')), may hold values from 0 to 8191, as said below
- block_team: int32 [32, 1], replicated, may hold values from 0 to 7; in each aligned block of 4 rows (0 to 3, 4 to 7, ...) at most 2 rows name the same one
- w_in: bfloat16 [8, 4, 1600, 24], P('team', 'member'), may hold values from -1.25 to 1.25
- w_mid: bfloat16 [8, 4, 800, 1600], P('team', 'member'), may hold values from -0.15625 to 0.15625
- w_low: bfloat16 [8, 4, 400, 800], P('team', 'member'), may hold values from -0.21875 to 0.21875
- w_out: bfloat16 [8, 4, 24, 400], P('team', 'member'), may hold values from -0.3125 to 0.3125
Outputs:
- source_rates: float32 [24, 512, 512], P(None, 'team', 'member')
- new_state: float32 [24, 512, 512], P(None, 'team', 'member')
Inputs may be any that keep to these rules, and one draw needn't show every extreme that they name: `flame_cells`: the 128 entries of the rows of one device (rows d * 1 to d + 1 - 1) are distinct cells of that device's tile, given as i * 128 + j. `block_team`: in each aligned block of 4 rows (the flame blocks of one index of team) no regime appears more than 2 times.
All inputs are finite; a program needn't handle non-finite values.
Results may differ from a plain program's by a relative error of at most 0.0017.
The roundings to bfloat16 on the way count: a program that leaves them out, or rounds other values in their place, can miss the bound.
Values may be sent and summed in bfloat16 or wider, within the bound.
A program may use at most 64 MiB of HBM per device.

v0:
```python
import math
import jax
import jax.numpy as jnp
from jax import lax
from jax.sharding import PartitionSpec as P

BLK_DEV = 1
CAP = 2
TIME_STEP = 0.25


def padded_2(block, sides, width):
    for axis, dim in sides:
        count = lax.axis_size(axis)
        forward = [(i, i + 1) for i in range(count - 1)]
        forward.append((count - 1, 0))
        backward = [(target, source) for source, target in forward]
        low = lax.ppermute(
            lax.slice_in_dim(block, block.shape[dim] - width, None, axis=dim), axis, forward
        )
        high = lax.ppermute(lax.slice_in_dim(block, 0, width, axis=dim), axis, backward)
        block = jnp.concatenate([low, block, high], axis=dim)
    return block


def build_slots(assigned, regimes, capacity):
    regime_ids = jnp.arange(regimes, dtype=jnp.int32)
    onehot = (assigned[:, None] == regime_ids[None, :]).astype(jnp.int32)
    ranks = jnp.sum((jnp.cumsum(onehot, axis=0) - onehot) * onehot, axis=1)
    slot_ids = jnp.arange(capacity, dtype=jnp.int32)
    row_ids = jnp.arange(assigned.shape[0], dtype=jnp.int32)
    match_regime = assigned[None, None, :] == regime_ids[:, None, None]
    match_rank = ranks[None, None, :] == slot_ids[None, :, None]
    matched = (match_regime & match_rank).astype(jnp.int32)
    slot_row = jnp.sum(matched * row_ids[None, None, :], axis=2)
    slot_valid = jnp.sum(matched, axis=2) > 0
    return (ranks, slot_row, slot_valid)


def shards(
    state_start,
    state_section,
    velocity,
    diffusivity,
    flame_cells,
    block_team,
    w_in,
    w_mid,
    w_low,
    w_out,
):
    regimes = lax.axis_size("team")
    members = lax.axis_size("member")
    fields, rows_x, rows_y = state_section.shape
    block_cells = flame_cells.shape[1]
    row_blocks = members * BLK_DEV
    slot_width = CAP * block_cells
    team_index = lax.axis_index("team")
    padded = padded_2(state_section.astype(jnp.bfloat16), (("team", 1), ("member", 2)), 1).astype(
        state_section.dtype
    )
    plus_x = padded[:, 2:, 1:-1]
    minus_x = padded[:, :-2, 1:-1]
    plus_y = padded[:, 1:-1, 2:]
    minus_y = padded[:, 1:-1, :-2]
    spread = diffusivity[:, None, None] * (
        plus_x + minus_x + plus_y + minus_y - 4.0 * state_section
    )
    advect = 0.5 * velocity[0][None] * (plus_x - minus_x) + 0.5 * velocity[1][None] * (
        plus_y - minus_y
    )
    flow = spread - advect
    assigned = lax.dynamic_slice_in_dim(block_team[:, 0], team_index * row_blocks, row_blocks)
    ranks, slot_row, slot_valid = build_slots(assigned, regimes, CAP)
    flat_section = state_section.reshape(fields, rows_x * rows_y)
    own_states = jnp.transpose(jnp.take(flat_section, flame_cells, axis=1), (1, 0, 2)).astype(
        jnp.bfloat16
    )
    row_states = lax.all_gather(own_states, "member", axis=0, tiled=True)
    picked = jnp.take(row_states, slot_row.reshape(-1), axis=0).reshape(
        regimes, CAP, fields, block_cells
    )
    picked = jnp.where(slot_valid[:, :, None, None], picked, jnp.zeros_like(picked))
    outgoing = jnp.transpose(picked, (0, 2, 1, 3)).reshape(regimes, fields, slot_width)
    incoming = lax.all_to_all(outgoing, "team", split_axis=0, concat_axis=0, tiled=True)
    weight_in = w_in[0, 0]
    weight_mid = w_mid[0, 0]
    weight_low = w_low[0, 0]
    weight_out = w_out[0, 0]
    group_size = math.gcd(regimes, max(1, 1024 // slot_width))
    grouped = incoming.reshape(regimes // group_size, group_size, fields, slot_width)

    def run_group(states):
        layer_one = jnp.einsum("hf,gfk->hgk", weight_in, states, preferred_element_type=jnp.float32)
        hidden_one = jax.nn.silu(layer_one).astype(jnp.bfloat16)
        layer_two = jnp.einsum(
            "ih,hgk->igk", weight_mid, hidden_one, preferred_element_type=jnp.float32
        )
        hidden_two = jax.nn.silu(layer_two).astype(jnp.bfloat16)
        layer_three = jnp.einsum(
            "ji,igk->jgk", weight_low, hidden_two, preferred_element_type=jnp.float32
        )
        hidden_three = jax.nn.silu(layer_three).astype(jnp.bfloat16)
        return jnp.einsum(
            "fj,jgk->gfk", weight_out, hidden_three, preferred_element_type=jnp.float32
        )

    produced = lax.map(run_group, grouped).reshape(regimes, fields, slot_width)
    returned = lax.all_to_all(produced, "team", split_axis=0, concat_axis=0, tiled=True)
    slot_rates = returned.reshape(regimes, fields, CAP, block_cells)
    row_terms = slot_rates[assigned, :, ranks]
    own_rates = lax.psum_scatter(row_terms, "member", scatter_dimension=0, tiled=True)
    flat_rates = jnp.zeros((fields, rows_x * rows_y), jnp.float32)
    flat_rates = flat_rates.at[:, flame_cells].add(jnp.transpose(own_rates, (1, 0, 2)))
    source_rates = flat_rates.reshape(fields, rows_x, rows_y)
    new_state = 0.75 * state_start + 0.25 * (state_section + TIME_STEP * (flow + source_rates))
    return (source_rates, new_state)


def solution(mesh):
    placed = (
        P(None, "team", "member"),
        P(None, "team", "member"),
        P(None, "team", "member"),
        P(),
        P(("team", "member"), None),
        P(),
        P("team", "member", None, None),
        P("team", "member", None, None),
        P("team", "member", None, None),
        P("team", "member", None, None),
    )
    return jax.shard_map(
        shards,
        mesh=mesh,
        in_specs=placed,
        out_specs=(P(None, "team", "member"), P(None, "team", "member")),
        check_vma=False,
    )
```

profile of v0, /device:TPU:0, one launch (start us, length us, event | category | flops | bytes accessed | tf_op | source)
XLA Modules:
  0.0 117.3 jit_solution(2329103246357906596)
XLA Ops:
  7.2 0.8 fusion.50
  10.3 2.8 %copy.52 = bf16[24,64,128]{0,2,1:T(8,128)(2,1)} copy(f32[24,64,128]{2,1,0:T(8,128)} %param.13) | data formatting | bytes 1179648 | tf_op args[1]
  13.0 2.5 %gather_fusion = bf16[128,24]{1,0:T(8,128)(2,1)S(1)} fusion(bf16[24,8192]{0,1:T(8,128)(2,1)} %bitcast.134, s32[1024]{0:T(1024)S(1)} %pad_clamp_fusion.1), kind=kCustom, calls=%fused_computation | custom fusion | bytes 12800 | tf_op jit(solution)/shard_map/jit(_take)/gather | solution.py:76
  15.7 9.7 %all_gather.3 = bf16[4,24,128]{2,1,0:T(8,128)(2,1)S(1)} all-gather(bf16[1,24,128]{2,1,0:T(8,128)(2,1)S(1)} %fusion.39), channel_id=1, replica_groups=mesh['team'=8,'member'=4] {'member'}, dimensions={0}, use_global_device_ids=true | all-gather | bytes 30720 | tf_op jit(solution)/shard_map/all_gather | solution.py:79
  26.8 4.9 %all-to-all-start = ((bf16[8,24,256]{2,1,0:T(8,128)(2,1)}), bf16[8,24,256]{2,1,0:T(8,128)(2,1)S(1)}, u32[]{:S(2)}, u32[]{:S(2)}) async-start(bf16[8,24,256]{2,1,0:T(8,128)(2,1)} %reshape.185), calls=%async_computation | async-start | bytes 196608 | tf_op jit(solution)/shard_map/all_to_all | solution.py:85
  32.3 3.1 %collective-permute-start.1 = (bf16[24,1,128]{2,1,0:T(2,128)(2,1)S(1)}, bf16[24,1,128]{2,1,0:T(2,128)(2,1)S(1)}, u32[]{:S(2)}, u32[]{:S(2)}) collective-permute-start(bf16[24,1,128]{2,1,0:T(2,128)(2,1)S(1)} %get-tuple-element.73), channel_id=1, source_target_pairs={{4,0},{8,4},{12,8},{16,12},{20,16},{24,20},{28,24},{0,28},{5,1},{9... | collective-permute-start | bytes 18440 | tf_op jit(solution)/shard_map/ppermute | solution.py:21
  35.5 2.6 %all-to-all-done = bf16[8,24,256]{2,1,0:T(8,128)(2,1)S(1)} async-done(((bf16[8,24,256]{2,1,0:T(8,128)(2,1)}), bf16[8,24,256]{2,1,0:T(8,128)(2,1)S(1)}, u32[]{:S(2)}, u32[]{:S(2)}) %all-to-all-start) | async-done | bytes 98336 | tf_op jit(solution)/shard_map/all_to_all | solution.py:85
  38.1 24.8 %while.10 = (s32[]{:T(128)}, f32[2,4,24,256]{3,2,1,0:T(8,128)}, bf16[2,4,24,256]{3,2,1,0:T(8,128)(2,1)S(1)}, bf16[1600,24]{0,1:T(8,128)(2,1)S(1)}, bf16[800,1600...) while((s32[]{:T(128)}, f32[2,4,24,256]{3,2,1,0:T(8,128)}, ...), condition=%wide.region_5.6_spmd, body=%wide.region_4.5_spmd.sunk | while | flops 3389440000 | bytes 10000729 | solution.py:108
  38.1 7.9 %fusion.71 = f32[4,256,800]{1,2,0:T(8,128)} fusion(bf16[800,1600]{1,0:T(8,128)(2,1)} %get-tuple-element.141, bf16[1600,24]{0,1:T(8,128)(2,1)S(1)} %get-tuple-element.140, bf16[2,4,24,256]{3,2,1,0:T(8,128)(2,1)S(1)} %get-tuple-element.139, s32[]{:T(128)} %get-tuple-element.129), kind=kOutput, calls=%fused_computation.16.clone.1 | convolution fusion | flops 2708275200 | bytes 5965828 | tf_op jit(solution)/shard_map/while/body/eval_jaxpr/ih,hgk->igk/dot_general | solution.py:96
  46.1 4.5 %fusion.72 = f32[2,4,24,256]{3,2,1,0:T(8,128)} fusion(f32[2,4,24,256]{3,2,1,0:T(8,128)} %get-tuple-element.130, s32[]{:T(128)} %get-tuple-element.129, f32[4,256,800]{1,2,0:T(8,128)} %fusion.71, bf16[400,800]{1,0:T(8,128)(2,1)S(1)} %get-tuple-element.142, bf16[24,400]{1,0:T(8,128)(2,1)S(1)} %get-tuple-element.143), kind=kOutput, calls=%fused_computation.26.clone.1 | convolution fusion | flops 681164800 | bytes 4034816 | tf_op jit(solution)/shard_map/while/body/eval_jaxpr/fj,jgk->gfk/dot_general | solution.py:104
  50.5 7.9 %fusion.71 = f32[4,256,800]{1,2,0:T(8,128)} fusion(bf16[800,1600]{1,0:T(8,128)(2,1)} %get-tuple-element.141, bf16[1600,24]{0,1:T(8,128)(2,1)S(1)} %get-tuple-element.140, bf16[2,4,24,256]{3,2,1,0:T(8,128)(2,1)S(1)} %get-tuple-element.139, s32[]{:T(128)} %get-tuple-element.129), kind=kOutput, calls=%fused_computation.16.clone.1 | convolution fusion | flops 2708275200 | bytes 5965828 | tf_op jit(solution)/shard_map/while/body/eval_jaxpr/ih,hgk->igk/dot_general | solution.py:96
  58.4 4.4 %fusion.72 = f32[2,4,24,256]{3,2,1,0:T(8,128)} fusion(f32[2,4,24,256]{3,2,1,0:T(8,128)} %get-tuple-element.130, s32[]{:T(128)} %get-tuple-element.129, f32[4,256,800]{1,2,0:T(8,128)} %fusion.71, bf16[400,800]{1,0:T(8,128)(2,1)S(1)} %get-tuple-element.142, bf16[24,400]{1,0:T(8,128)(2,1)S(1)} %get-tuple-element.143), kind=kOutput, calls=%fused_computation.26.clone.1 | convolution fusion | flops 681164800 | bytes 4034816 | tf_op jit(solution)/shard_map/while/body/eval_jaxpr/fj,jgk->gfk/dot_general | solution.py:104
  62.9 3.4 %all-to-all-start.1 = ((f32[8,24,256]{2,1,0:T(8,128)}), f32[8,24,256]{2,1,0:T(8,128)S(1)}, u32[]{:S(2)}, u32[]{:S(2)}) async-start(f32[8,24,256]{2,1,0:T(8,128)} %bitcast.24), calls=%async_computation.1 | async-start | bytes 393216 | tf_op jit(solution)/shard_map/all_to_all | solution.py:109
  66.7 1.5 %collective-permute-start.2 = (bf16[24,66,1]{2,1,0:T(8,128)(2,1)S(1)}, bf16[24,66,1]{2,1,0:T(8,128)(2,1)S(1)}, u32[]{:S(2)}, u32[]{:S(2)}) collective-permute-start(bf16[24,66,1]{2,1,0:T(8,128)(2,1)S(1)} %get-tuple-element.70), channel_id=1, source_target_pairs={{0,1},{1,2},{2,3},{3,0},{4,5},{5,6},{6,7},{7,4},{8,9},{9,10},{10,1... | collective-permute-start | bytes 9512 | tf_op jit(solution)/shard_map/ppermute | solution.py:18
  68.3 1.4 %collective-permute-start.3 = (bf16[24,66,1]{2,1,0:T(8,128)(2,1)S(1)}, bf16[24,66,1]{2,1,0:T(8,128)(2,1)}, u32[]{:S(2)}, u32[]{:S(2)}) collective-permute-start(bf16[24,66,1]{2,1,0:T(8,128)(2,1)S(1)} %get-tuple-element.71), channel_id=1, source_target_pairs={{1,0},{2,1},{3,2},{0,3},{5,4},{6,5},{7,6},{4,7},{9,8},{10,9},{11,1... | collective-permute-start | bytes 9512 | tf_op jit(solution)/shard_map/ppermute | solution.py:21
  69.7 4.8 %all-to-all-done.1 = f32[8,24,256]{2,1,0:T(8,128)S(1)} async-done(((f32[8,24,256]{2,1,0:T(8,128)}), f32[8,24,256]{2,1,0:T(8,128)S(1)}, u32[]{:S(2)}, u32[]{:S(2)}) %all-to-all-start.1) | async-done | bytes 196640 | tf_op jit(solution)/shard_map/all_to_all | solution.py:109
  74.5 1.2 %gather_fusion.2 = f32[4,24,128]{2,1,0:T(8,128)} fusion(f32[8,24,2,128]{3,1,2,0:T(8,128)S(1)} %copy_bitcast_fusion, s32[4]{0:T(128)S(1)} %fusion.49), kind=kCustom, calls=%fused_computation.2 | custom fusion | bytes 98336 | tf_op jit(solution)/shard_map/gather | solution.py:111
  75.7 5.0 %collective-permute-done.2 = bf16[24,66,1]{2,1,0:T(8,128)(2,1)S(1)} collective-permute-done((bf16[24,66,1]{2,1,0:T(8,128)(2,1)S(1)}, bf16[24,66,1]{2,1,0:T(8,128)(2,1)S(1)}, u32[]{:S(2)}, u32[]{:S(2)}) %collective-permute-start.2) | collective-permute-done | bytes 3200 | tf_op jit(solution)/shard_map/ppermute | solution.py:18
  80.7 9.3 %collective-permute-done.3 = bf16[24,66,1]{2,1,0:T(8,128)(2,1)} collective-permute-done((bf16[24,66,1]{2,1,0:T(8,128)(2,1)S(1)}, bf16[24,66,1]{2,1,0:T(8,128)(2,1)}, u32[]{:S(2)}, u32[]{:S(2)}) %collective-permute-start.3) | collective-permute-done | bytes 3200 | tf_op jit(solution)/shard_map/ppermute | solution.py:21
  90.0 1.7 %maximum_convert_fusion = f32[24,66,130]{2,1,0:T(8,128)S(1)} fusion(bf16[24,66,1]{2,1,0:T(8,128)(2,1)} %collective-permute-done.3, bf16[24,1,128]{2,1,0:T(2,128)(2,1)S(1)} %collective-permute-done.1, bf16[24,64,128]{2,1,0:T(8,128)(2,1)S(1)} %convert_element_type.35, bf16[24,1,128]{2,1,0:T(2,128)(2,1)S(1)} %collective-permute-done, ...), kind=kLoop, calls=%fused_computation.37 | loop fusion | flops 2059200 | bytes 1235520 | tf_op jit(solution)/shard_map/convert_element_type | solution.py:59
  91.7 8.6 %reduce-scatter.4.cloned.1.call-done = f32[1,24,128]{2,1,0:T(8,128)} async-done(((f32[4,24,128]{2,1,0:T(8,128)}), f32[1,24,128]{2,1,0:T(8,128)}) %reduce-scatter.4.cloned.1.call-update) | async-done | bytes 12304
  101.1 3.2 %scatter_custom_fusion = f32[24,8192]{0,1:T(8,128)} fusion(s32[128]{0:T(128)S(1)} %fusion.51, f32[128,24]{1,0:T(8,128)S(1)} %copy.57, f32[]{:T(128)} %constant.35.clone.1), kind=kCustom, calls=%fused_computation.35 | custom fusion | flops 3072 | bytes 786436 | tf_op jit(solution)/shard_map/scatter-add | solution.py:114
  104.3 2.9 %copy.59 = f32[24,64,128]{2,1,0:T(8,128)S(1)} copy(f32[24,64,128]{0,2,1:T(8,128)} %bitcast.133) | data formatting | bytes 1572864
  107.3 3.2 %multiply_add_fusion = f32[24,64,128]{2,1,0:T(8,128)} fusion(f32[24,64,128]{2,1,0:T(8,128)S(1)} %copy-done, f32[24,64,128]{2,1,0:T(8,128)S(1)} %copy.59, f32[24,66,130]{2,1,0:T(8,128)S(1)} %maximum_convert_fusion, f32[24,64,128]{2,1,0:T(8,128)} %param.12, f32[64,128]{1,0:T(8,128)S(1)} %get-tuple-element.75, f32[64,128]{1,0:T(8,128)S(1)} %get-tuple-element.74, ...), kind=kLoop, calls=%fused_computation.38 | loop fusion | flops 3538944 | bytes 6357088 | tf_op jit(solution)/shard_map/add | solution.py:116
  (51 shorter events, 5.7 us)
Async XLA Ops:
  7.2 28.3 %copy-start.4 = (s32[32,1]{0,1:T(1,128)S(1)}, s32[32,1]{0,1:T(1,128)}, u32[]{:S(2)}) copy-start(s32[32,1]{0,1:T(1,128)} %param.17) | copy-start | bytes 388
  7.2 24.5 %copy-start = (f32[24,64,128]{2,1,0:T(8,128)S(1)}, f32[24,64,128]{2,1,0:T(8,128)}, u32[]{:S(2)}) copy-start(f32[24,64,128]{2,1,0:T(8,128)} %param.13) | copy-start | bytes 2359300
  7.2 28.2 %copy-start.2 = (f32[2,64,128]{2,1,0:T(8,128)S(1)}, f32[2,64,128]{2,1,0:T(8,128)}, u32[]{:S(2)}) copy-start(f32[2,64,128]{2,1,0:T(8,128)} %param.14) | copy-start | bytes 196612
  7.2 30.9 %copy-start.6 = (bf16[1,1,1600,24]{2,3,1,0:T(8,128)(2,1)S(1)}, bf16[1,1,1600,24]{2,3,1,0:T(8,128)(2,1)}, u32[]{:S(2)}) copy-start(bf16[1,1,1600,24]{2,3,1,0:T(8,128)(2,1)} %param.18) | copy-start | bytes 230404
  7.2 30.9 %copy-start.5 = (bf16[1,1,400,800]{3,2,1,0:T(8,128)(2,1)S(1)}, bf16[1,1,400,800]{3,2,1,0:T(8,128)(2,1)}, u32[]{:S(2)}) copy-start(bf16[1,1,400,800]{3,2,1,0:T(8,128)(2,1)} %param.20) | copy-start | bytes 1920004
  7.2 30.9 %copy-start.7 = (bf16[1,1,24,400]{3,2,1,0:T(8,128)(2,1)S(1)}, bf16[1,1,24,400]{3,2,1,0:T(8,128)(2,1)}, u32[]{:S(2)}) copy-start(bf16[1,1,24,400]{3,2,1,0:T(8,128)(2,1)} %param.21) | copy-start | bytes 57604
  26.8 11.3 %all-to-all-start = ((bf16[8,24,256]{2,1,0:T(8,128)(2,1)}), bf16[8,24,256]{2,1,0:T(8,128)(2,1)S(1)}, u32[]{:S(2)}, u32[]{:S(2)}) async-start(bf16[8,24,256]{2,1,0:T(8,128)(2,1)} %reshape.185), calls=%async_computation | async-start | bytes 196608 | tf_op jit(solution)/shard_map/all_to_all | solution.py:85
  31.8 34.6 %collective-permute-start = (bf16[24,1,128]{2,1,0:T(2,128)(2,1)S(1)}, bf16[24,1,128]{2,1,0:T(2,128)(2,1)S(1)}, u32[]{:S(2)}, u32[]{:S(2)}) collective-permute-start(bf16[24,1,128]{2,1,0:T(2,128)(2,1)S(1)} %get-tuple-element.72), channel_id=1, source_target_pairs={{0,4},{4,8},{8,12},{12,16},{16,20},{20,24},{24,28},{28,0},{1,5},{5... | collective-permute-start | bytes 18440 | tf_op jit(solution)/shard_map/ppermute | solution.py:18
  32.3 34.0 %collective-permute-start.1 = (bf16[24,1,128]{2,1,0:T(2,128)(2,1)S(1)}, bf16[24,1,128]{2,1,0:T(2,128)(2,1)S(1)}, u32[]{:S(2)}, u32[]{:S(2)}) collective-permute-start(bf16[24,1,128]{2,1,0:T(2,128)(2,1)S(1)} %get-tuple-element.73), channel_id=1, source_target_pairs={{4,0},{8,4},{12,8},{16,12},{20,16},{24,20},{28,24},{0,28},{5,1},{9... | collective-permute-start | bytes 18440 | tf_op jit(solution)/shard_map/ppermute | solution.py:21
  62.9 11.6 %all-to-all-start.1 = ((f32[8,24,256]{2,1,0:T(8,128)}), f32[8,24,256]{2,1,0:T(8,128)S(1)}, u32[]{:S(2)}, u32[]{:S(2)}) async-start(f32[8,24,256]{2,1,0:T(8,128)} %bitcast.24), calls=%async_computation.1 | async-start | bytes 393216 | tf_op jit(solution)/shard_map/all_to_all | solution.py:109
  66.3 34.0 %reduce-scatter.4.cloned.1.call-start = ((), (), s32[]{:S(2)}) async-start(), calls=%async_computation.3 | async-start | bytes 61440
  66.7 14.0 %collective-permute-start.2 = (bf16[24,66,1]{2,1,0:T(8,128)(2,1)S(1)}, bf16[24,66,1]{2,1,0:T(8,128)(2,1)S(1)}, u32[]{:S(2)}, u32[]{:S(2)}) collective-permute-start(bf16[24,66,1]{2,1,0:T(8,128)(2,1)S(1)} %get-tuple-element.70), channel_id=1, source_target_pairs={{0,1},{1,2},{2,3},{3,0},{4,5},{5,6},{6,7},{7,4},{8,9},{9,10},{10,1... | collective-permute-start | bytes 9512 | tf_op jit(solution)/shard_map/ppermute | solution.py:18
  68.3 21.7 %collective-permute-start.3 = (bf16[24,66,1]{2,1,0:T(8,128)(2,1)S(1)}, bf16[24,66,1]{2,1,0:T(8,128)(2,1)}, u32[]{:S(2)}, u32[]{:S(2)}) collective-permute-start(bf16[24,66,1]{2,1,0:T(8,128)(2,1)S(1)} %get-tuple-element.71), channel_id=1, source_target_pairs={{1,0},{2,1},{3,2},{0,3},{5,4},{6,5},{7,6},{4,7},{9,8},{10,9},{11,1... | collective-permute-start | bytes 9512 | tf_op jit(solution)/shard_map/ppermute | solution.py:21
  104.3 3.0 %copy-start.3 = (f32[24]{0:T(128)S(1)}, f32[24]{0:T(128)}, u32[]{:S(2)}) copy-start(f32[24]{0:T(128)} %param.15) | copy-start | bytes 292
  107.3 3.2 %copy-start.1 = (f32[24,64,128]{2,1,0:T(8,128)}, f32[24,64,128]{2,1,0:T(8,128)S(1)}, u32[]{:S(2)}) copy-start(f32[24,64,128]{2,1,0:T(8,128)S(1)} %copy.59) | copy-start | bytes 2359300
Sparse Core Ops, SparseCore 0:
  75.9 24.4 reduce-scatter.3
where the time goes:
time: 118 us; the launch traced here: 117 us
  waiting for transfers between devices  30.3 us (26%)
  matrix products  24.8 us (21%)
  starting transfers between devices  14.9 us (13%)
  between operations  14.2 us (12%)
  local copies, waits for them, and re-layouts  13 us (11%)
  other arithmetic  10.4 us (9%)
  blocking collectives  9.67 us (8%)
    dot_general x2, matrix products, run_group(): jnp.einsum('ih,hgk->igk', weight_mid, hidden_one, preferred_element_type=...  15.9 us
    all_gather x1, blocking collectives, shards(): row_states = lax.all_gather(own_states, 'member', axis=0, tiled=True)  9.67 us
    ppermute x2, waiting for transfers between devices, padded_2(): lax.ppermute(lax.slice_in_dim(block, 0, width, axis=dim), axis, backward)  9.28 us
    dot_general x2, matrix products, run_group(): jnp.einsum('fj,jgk->gfk', weight_out, hidden_three, preferred_element_typ...  8.9 us
    unnamed x2, waiting for transfers between devices  8.64 us
    unnamed x18, local copies, waits for them, and re-layouts  5.76 us
    ppermute x2, waiting for transfers between devices, padded_2(): lax.ppermute(lax.slice_in_dim(block, block.shape[dim] - width, None, axis...  4.99 us
    all_to_all x1, starting transfers between devices, shards(): lax.all_to_all(outgoing, 'team', split_axis=0, concat_axis=0, tiled=True)  4.88 us
  transfers between devices with their start and end apart: 7, of which 5 were waited for; matrix products, arithmetic and copies ran while one was open for 24% of the time, Pallas kernels for 0%

commit v1 on v0

--- a/solution.py
+++ b/solution.py
@@ -82,7 +82,18 @@
     )
     picked = jnp.where(slot_valid[:, :, None, None], picked, jnp.zeros_like(picked))
     outgoing = jnp.transpose(picked, (0, 2, 1, 3)).reshape(regimes, fields, slot_width)
-    incoming = lax.all_to_all(outgoing, "team", split_axis=0, concat_axis=0, tiled=True)
+    ways, here = (lax.axis_size("team"), lax.axis_index("team"))
+    width_2 = outgoing.shape[0] // ways
+    dims = list(outgoing.shape)
+    dims[0] = width_2
+    height = dims[0]
+    dims[0] = height * ways
+    incoming = jnp.zeros(dims, outgoing.dtype)
+    for mask in range(ways):
+        part = lax.dynamic_slice_in_dim(outgoing, (here ^ mask) * width_2, width_2, axis=0)
+        if mask:
+            part = lax.ppermute(part, "team", [(d, d ^ mask) for d in range(ways)])
+        incoming = lax.dynamic_update_slice_in_dim(incoming, part, (here ^ mask) * height, axis=0)
     weight_in = w_in[0, 0]
     weight_mid = w_mid[0, 0]
     weight_low = w_low[0, 0]

time: 118 us -> 119 us (level)
  starting transfers between devices: 14.9 us -> 17.4 us
  waiting for transfers between devices: 30.3 us -> 28.9 us
    ppermute x0 -> x7, starting transfers between devices: none -> 8.31 us  [shards(): part = lax.ppermute(part, 'team', [(d, d ^ mask) for d in range(ways)])]
    ppermute x2, waiting for transfers between devices: 4.99 us -> 10.2 us  [padded_2(): lax.ppermute(lax.slice_in_dim(block, block.shape[dim] - width, None, axis...]
    ppermute x2, waiting for transfers between devices: 9.28 us -> 4.09 us  [padded_2(): lax.ppermute(lax.slice_in_dim(block, 0, width, axis=dim), axis, backward)]
    all_to_all x1 -> x0, starting transfers between devices: 4.88 us -> none  [shards(): lax.all_to_all(outgoing, 'team', split_axis=0, concat_axis=0, tiled=True)]
    all_to_all x1 -> x0, waiting for transfers between devices: 2.57 us -> none  [shards(): lax.all_to_all(outgoing, 'team', split_axis=0, concat_axis=0, tiled=True)]
    ppermute x2, starting transfers between devices: 2.1 us -> 0.74 us  [padded_2(): lax.ppermute(lax.slice_in_dim(block, block.shape[dim] - width, None, axis...]
    ppermute x0 -> x7, waiting for transfers between devices: none -> 1.2 us  [shards(): part = lax.ppermute(part, 'team', [(d, d ^ mask) for d in range(ways)])]
  transfers between devices with their start and end apart: 7 -> 13, of which waited for: 5 -> 5; matrix products, arithmetic and copies ran while one was open for 24% -> 24% of each run, Pallas kernels for 0% -> 0%
where the time goes in v1:
time: 119 us; the launch traced here: 118 us
  waiting for transfers between devices  28.9 us (24%)
  matrix products  24.8 us (21%)
  starting transfers between devices  17.4 us (15%)
  between operations  14.3 us (12%)
  local copies, waits for them, and re-layouts  12.5 us (11%)
  other arithmetic  10.4 us (9%)
  blocking collectives  9.67 us (8%)
    dot_general x2, matrix products, run_group(): jnp.einsum('ih,hgk->igk', weight_mid, hidden_one, preferred_element_type=...  15.9 us
    ppermute x2, waiting for transfers between devices, padded_2(): lax.ppermute(lax.slice_in_dim(block, block.shape[dim] - width, None, axis...  10.2 us
    all_gather x1, blocking collectives, shards(): row_states = lax.all_gather(own_states, 'member', axis=0, tiled=True)  9.67 us
    dot_general x2, matrix products, run_group(): jnp.einsum('fj,jgk->gfk', weight_out, hidden_three, preferred_element_typ...  8.89 us
    ppermute x7, starting transfers between devices, shards(): part = lax.ppermute(part, 'team', [(d, d ^ mask) for d in range(ways)])  8.31 us
    unnamed x2, waiting for transfers between devices  7.77 us
    unnamed x18, local copies, waits for them, and re-layouts  5.8 us
    all_to_all x1, waiting for transfers between devices, shards(): lax.all_to_all(produced, 'team', split_axis=0, concat_axis=0, tiled=True)  5.7 us
  transfers between devices with their start and end apart: 13, of which 5 were waited for; matrix products, arithmetic and copies ran while one was open for 24% of the time, Pallas kernels for 0%

profile of v1, /device:TPU:0, one launch (start us, length us, event | category | flops | bytes accessed | tf_op | source)
XLA Modules:
  0.0 118.0 jit_solution(5070818084811160119)
XLA Ops:
  10.2 2.8 %copy.73 = bf16[24,64,128]{0,2,1:T(8,128)(2,1)} copy(f32[24,64,128]{2,1,0:T(8,128)} %param.13) | data formatting | bytes 1179648 | tf_op args[1]
  13.0 2.5 %gather_fusion = bf16[128,24]{1,0:T(8,128)(2,1)S(1)} fusion(bf16[24,8192]{0,1:T(8,128)(2,1)} %bitcast.134, s32[1024]{0:T(1024)S(1)} %pad_clamp_fusion.1), kind=kCustom, calls=%fused_computation | custom fusion | bytes 12800 | tf_op jit(solution)/shard_map/jit(_take)/gather | solution.py:76
  15.6 9.7 %all_gather.3 = bf16[4,24,128]{2,1,0:T(8,128)(2,1)S(1)} all-gather(bf16[1,24,128]{2,1,0:T(8,128)(2,1)S(1)} %fusion.39), channel_id=1, replica_groups=mesh['team'=8,'member'=4] {'member'}, dimensions={0}, use_global_device_ids=true | all-gather | bytes 30720 | tf_op jit(solution)/shard_map/all_gather | solution.py:79
  26.3 1.6 %collective-permute-start.1 = (bf16[1,24,256]{2,1,0:T(8,128)(2,1)S(1)}, bf16[1,24,256]{2,1,0:T(8,128)(2,1)S(1)}, u32[]{:S(2)}, u32[]{:S(2)}) collective-permute-start(bf16[1,24,256]{2,1,0:T(8,128)(2,1)S(1)} %get-tuple-element.79), channel_id=1, source_target_pairs={{0,8},{4,12},{8,0},{12,4},{16,24},{20,28},{24,16},{28,20},{1,9},{5... | collective-permute-start | bytes 36872 | tf_op jit(solution)/shard_map/ppermute | solution.py:95
  28.2 2.6 %collective-permute-start.3 = (bf16[1,24,256]{2,1,0:T(8,128)(2,1)S(1)}, bf16[1,24,256]{2,1,0:T(8,128)(2,1)S(1)}, u32[]{:S(2)}, u32[]{:S(2)}) collective-permute-start(bf16[1,24,256]{2,1,0:T(8,128)(2,1)S(1)} %get-tuple-element.77), channel_id=1, source_target_pairs={{0,16},{4,20},{8,24},{12,28},{16,0},{20,4},{24,8},{28,12},{1,17},{... | collective-permute-start | bytes 36872 | tf_op jit(solution)/shard_map/ppermute | solution.py:95
  31.0 3.6 %collective-permute-start.5 = (bf16[1,24,256]{2,1,0:T(8,128)(2,1)S(1)}, bf16[1,24,256]{2,1,0:T(8,128)(2,1)S(1)}, u32[]{:S(2)}, u32[]{:S(2)}) collective-permute-start(bf16[1,24,256]{2,1,0:T(8,128)(2,1)S(1)} %get-tuple-element.75), channel_id=1, source_target_pairs={{0,24},{4,28},{8,16},{12,20},{16,8},{20,12},{24,0},{28,4},{1,25},{... | collective-permute-start | bytes 36872 | tf_op jit(solution)/shard_map/ppermute | solution.py:95
  35.0 3.3 %collective-permute-start.8 = (bf16[24,1,128]{2,1,0:T(2,128)(2,1)S(1)}, bf16[24,1,128]{2,1,0:T(2,128)(2,1)S(1)}, u32[]{:S(2)}, u32[]{:S(2)}) collective-permute-start(bf16[24,1,128]{2,1,0:T(2,128)(2,1)S(1)} %get-tuple-element.73), channel_id=1, source_target_pairs={{4,0},{8,4},{12,8},{16,12},{20,16},{24,20},{28,24},{0,28},{5,1},{9... | collective-permute-start | bytes 18440 | tf_op jit(solution)/shard_map/ppermute | solution.py:21
  38.4 1.2 %collective-permute-done.6 = bf16[1,24,256]{2,1,0:T(8,128)(2,1)S(1)} collective-permute-done((bf16[1,24,256]{2,1,0:T(8,128)(2,1)S(1)}, bf16[1,24,256]{2,1,0:T(8,128)(2,1)S(1)}, u32[]{:S(2)}, u32[]{:S(2)}) %collective-permute-start.6) | collective-permute-done | bytes 12320 | tf_op jit(solution)/shard_map/ppermute | solution.py:95
  39.6 24.8 %while.10 = (s32[]{:T(128)}, f32[2,4,24,256]{3,2,1,0:T(8,128)}, bf16[2,4,24,256]{3,2,1,0:T(8,128)(2,1)S(1)}, bf16[1600,24]{0,1:T(8,128)(2,1)S(1)}, bf16[800,1600...) while((s32[]{:T(128)}, f32[2,4,24,256]{3,2,1,0:T(8,128)}, ...), condition=%wide.region_5.6_spmd, body=%wide.region_4.5_spmd.sunk | while | flops 3389440000 | bytes 10000729 | solution.py:119
  39.6 7.9 %fusion.71 = f32[4,256,800]{1,2,0:T(8,128)} fusion(bf16[800,1600]{1,0:T(8,128)(2,1)} %get-tuple-element.149, bf16[1600,24]{0,1:T(8,128)(2,1)S(1)} %get-tuple-element.148, bf16[2,4,24,256]{3,2,1,0:T(8,128)(2,1)S(1)} %get-tuple-element.147, s32[]{:T(128)} %get-tuple-element.137), kind=kOutput, calls=%fused_computation.16.clone.1 | convolution fusion | flops 2708275200 | bytes 5965828 | tf_op jit(solution)/shard_map/while/body/eval_jaxpr/ih,hgk->igk/dot_general | solution.py:107
  47.5 4.4 %fusion.72 = f32[2,4,24,256]{3,2,1,0:T(8,128)} fusion(f32[2,4,24,256]{3,2,1,0:T(8,128)} %get-tuple-element.138, s32[]{:T(128)} %get-tuple-element.137, f32[4,256,800]{1,2,0:T(8,128)} %fusion.71, bf16[400,800]{1,0:T(8,128)(2,1)S(1)} %get-tuple-element.150, bf16[24,400]{1,0:T(8,128)(2,1)S(1)} %get-tuple-element.151), kind=kOutput, calls=%fused_computation.26.clone.1 | convolution fusion | flops 681164800 | bytes 4034816 | tf_op jit(solution)/shard_map/while/body/eval_jaxpr/fj,jgk->gfk/dot_general | solution.py:115
  52.0 7.9 %fusion.71 = f32[4,256,800]{1,2,0:T(8,128)} fusion(bf16[800,1600]{1,0:T(8,128)(2,1)} %get-tuple-element.149, bf16[1600,24]{0,1:T(8,128)(2,1)S(1)} %get-tuple-element.148, bf16[2,4,24,256]{3,2,1,0:T(8,128)(2,1)S(1)} %get-tuple-element.147, s32[]{:T(128)} %get-tuple-element.137), kind=kOutput, calls=%fused_computation.16.clone.1 | convolution fusion | flops 2708275200 | bytes 5965828 | tf_op jit(solution)/shard_map/while/body/eval_jaxpr/ih,hgk->igk/dot_general | solution.py:107
  59.9 4.5 %fusion.72 = f32[2,4,24,256]{3,2,1,0:T(8,128)} fusion(f32[2,4,24,256]{3,2,1,0:T(8,128)} %get-tuple-element.138, s32[]{:T(128)} %get-tuple-element.137, f32[4,256,800]{1,2,0:T(8,128)} %fusion.71, bf16[400,800]{1,0:T(8,128)(2,1)S(1)} %get-tuple-element.150, bf16[24,400]{1,0:T(8,128)(2,1)S(1)} %get-tuple-element.151), kind=kOutput, calls=%fused_computation.26.clone.1 | convolution fusion | flops 681164800 | bytes 4034816 | tf_op jit(solution)/shard_map/while/body/eval_jaxpr/fj,jgk->gfk/dot_general | solution.py:115
  64.4 3.4 %all-to-all-start = ((f32[8,24,256]{2,1,0:T(8,128)}), f32[8,24,256]{2,1,0:T(8,128)S(1)}, u32[]{:S(2)}, u32[]{:S(2)}) async-start(f32[8,24,256]{2,1,0:T(8,128)} %bitcast.24), calls=%async_computation | async-start | bytes 393216 | tf_op jit(solution)/shard_map/all_to_all | solution.py:120
  68.2 1.5 %collective-permute-start.10 = (bf16[24,66,1]{2,1,0:T(8,128)(2,1)S(1)}, bf16[24,66,1]{2,1,0:T(8,128)(2,1)S(1)}, u32[]{:S(2)}, u32[]{:S(2)}) collective-permute-start(bf16[24,66,1]{2,1,0:T(8,128)(2,1)S(1)} %get-tuple-element.71), channel_id=1, source_target_pairs={{1,0},{2,1},{3,2},{0,3},{5,4},{6,5},{7,6},{4,7},{9,8},{10,9},{11,1... | collective-permute-start | bytes 9512 | tf_op jit(solution)/shard_map/ppermute | solution.py:21
  70.3 5.7 %all-to-all-done = f32[8,24,256]{2,1,0:T(8,128)S(1)} async-done(((f32[8,24,256]{2,1,0:T(8,128)}), f32[8,24,256]{2,1,0:T(8,128)S(1)}, u32[]{:S(2)}, u32[]{:S(2)}) %all-to-all-start) | async-done | bytes 196640 | tf_op jit(solution)/shard_map/all_to_all | solution.py:120
  76.0 1.2 gather_fusion.2
  77.2 4.1 %collective-permute-done.10 = bf16[24,66,1]{2,1,0:T(8,128)(2,1)S(1)} collective-permute-done((bf16[24,66,1]{2,1,0:T(8,128)(2,1)S(1)}, bf16[24,66,1]{2,1,0:T(8,128)(2,1)S(1)}, u32[]{:S(2)}, u32[]{:S(2)}) %collective-permute-start.10) | collective-permute-done | bytes 3200 | tf_op jit(solution)/shard_map/ppermute | solution.py:21
  81.3 10.2 %collective-permute-done.9 = bf16[24,66,1]{2,1,0:T(8,128)(2,1)} collective-permute-done((bf16[24,66,1]{2,1,0:T(8,128)(2,1)S(1)}, bf16[24,66,1]{2,1,0:T(8,128)(2,1)}, u32[]{:S(2)}, u32[]{:S(2)}) %collective-permute-start.9) | collective-permute-done | bytes 3200 | tf_op jit(solution)/shard_map/ppermute | solution.py:18
  91.5 1.7 %maximum_convert_fusion = f32[24,66,130]{2,1,0:T(8,128)S(1)} fusion(bf16[24,66,1]{2,1,0:T(8,128)(2,1)S(1)} %collective-permute-done.10, bf16[24,1,128]{2,1,0:T(2,128)(2,1)S(1)} %collective-permute-done.8, bf16[24,64,128]{2,1,0:T(8,128)(2,1)S(1)} %convert_element_type.35, bf16[24,1,128]{2,1,0:T(2,128)(2,1)S(1)} %collective-permute-done.7, ...), kind=kLoop, calls=%fused_computation.37 | loop fusion | flops 2059200 | bytes 1235520 | tf_op jit(solution)/shard_map/convert_element_type | solution.py:59
  93.2 7.8 %reduce-scatter.4.cloned.1.call-done = f32[1,24,128]{2,1,0:T(8,128)} async-done(((f32[4,24,128]{2,1,0:T(8,128)}), f32[1,24,128]{2,1,0:T(8,128)}) %reduce-scatter.4.cloned.1.call-update) | async-done | bytes 12304
  101.7 3.2 %scatter_custom_fusion = f32[24,8192]{0,1:T(8,128)} fusion(s32[128]{0:T(128)S(1)} %fusion.51, f32[128,24]{1,0:T(8,128)S(1)} %copy.78, f32[]{:T(128)} %constant.30.clone.1), kind=kCustom, calls=%fused_computation.35 | custom fusion | flops 3072 | bytes 786436 | tf_op jit(solution)/shard_map/scatter-add | solution.py:125
  104.9 2.9 %copy.80 = f32[24,64,128]{2,1,0:T(8,128)S(1)} copy(f32[24,64,128]{0,2,1:T(8,128)} %bitcast.133) | data formatting | bytes 1572864
  107.9 3.2 %multiply_add_fusion = f32[24,64,128]{2,1,0:T(8,128)} fusion(f32[24,64,128]{2,1,0:T(8,128)S(1)} %copy-done, f32[24,64,128]{2,1,0:T(8,128)S(1)} %copy.80, f32[24,66,130]{2,1,0:T(8,128)S(1)} %maximum_convert_fusion, f32[24,64,128]{2,1,0:T(8,128)} %param.12, f32[64,128]{1,0:T(8,128)S(1)} %get-tuple-element.83, f32[64,128]{1,0:T(8,128)S(1)} %get-tuple-element.82, ...), kind=kLoop, calls=%fused_computation.38 | loop fusion | flops 3538944 | bytes 6357088 | tf_op jit(solution)/shard_map/add | solution.py:127
  (72 shorter events, 6.6 us)
Async XLA Ops:
  7.2 23.6 %copy-start = (f32[24,64,128]{2,1,0:T(8,128)S(1)}, f32[24,64,128]{2,1,0:T(8,128)}, u32[]{:S(2)}) copy-start(f32[24,64,128]{2,1,0:T(8,128)} %param.13) | copy-start | bytes 2359300
  7.2 23.7 %copy-start.2 = (f32[2,64,128]{2,1,0:T(8,128)S(1)}, f32[2,64,128]{2,1,0:T(8,128)}, u32[]{:S(2)}) copy-start(f32[2,64,128]{2,1,0:T(8,128)} %param.14) | copy-start | bytes 196612
  9.9 21.0 %copy-start.4 = (s32[32,1]{0,1:T(1,128)S(1)}, s32[32,1]{0,1:T(1,128)}, u32[]{:S(2)}) copy-start(s32[32,1]{0,1:T(1,128)} %param.17) | copy-start | bytes 388
  10.2 29.4 %copy-start.5 = (bf16[1,1,400,800]{3,2,1,0:T(8,128)(2,1)S(1)}, bf16[1,1,400,800]{3,2,1,0:T(8,128)(2,1)}, u32[]{:S(2)}) copy-start(bf16[1,1,400,800]{3,2,1,0:T(8,128)(2,1)} %param.20) | copy-start | bytes 1920004
  10.2 29.4 %copy-start.6 = (bf16[1,1,1600,24]{2,3,1,0:T(8,128)(2,1)S(1)}, bf16[1,1,1600,24]{2,3,1,0:T(8,128)(2,1)}, u32[]{:S(2)}) copy-start(bf16[1,1,1600,24]{2,3,1,0:T(8,128)(2,1)} %param.18) | copy-start | bytes 230404
  10.2 29.4 %copy-start.7 = (bf16[1,1,24,400]{3,2,1,0:T(8,128)(2,1)S(1)}, bf16[1,1,24,400]{3,2,1,0:T(8,128)(2,1)}, u32[]{:S(2)}) copy-start(bf16[1,1,24,400]{3,2,1,0:T(8,128)(2,1)} %param.21) | copy-start | bytes 57604
  26.2 4.8 %collective-permute-start = (bf16[1,24,256]{2,1,0:T(8,128)(2,1)S(1)}, bf16[1,24,256]{2,1,0:T(8,128)(2,1)S(1)}, u32[]{:S(2)}, u32[]{:S(2)}) collective-permute-start(bf16[1,24,256]{2,1,0:T(8,128)(2,1)S(1)} %get-tuple-element.80), channel_id=1, source_target_pairs={{0,4},{4,0},{8,12},{12,8},{16,20},{20,16},{24,28},{28,24},{1,5},{5... | collective-permute-start | bytes 36872 | tf_op jit(solution)/shard_map/ppermute | solution.py:95
  26.3 8.3 %collective-permute-start.1 = (bf16[1,24,256]{2,1,0:T(8,128)(2,1)S(1)}, bf16[1,24,256]{2,1,0:T(8,128)(2,1)S(1)}, u32[]{:S(2)}, u32[]{:S(2)}) collective-permute-start(bf16[1,24,256]{2,1,0:T(8,128)(2,1)S(1)} %get-tuple-element.79), channel_id=1, source_target_pairs={{0,8},{4,12},{8,0},{12,4},{16,24},{20,28},{24,16},{28,20},{1,9},{5... | collective-permute-start | bytes 36872 | tf_op jit(solution)/shard_map/ppermute | solution.py:95
  28.0 6.8 %collective-permute-start.2 = (bf16[1,24,256]{2,1,0:T(8,128)(2,1)S(1)}, bf16[1,24,256]{2,1,0:T(8,128)(2,1)S(1)}, u32[]{:S(2)}, u32[]{:S(2)}) collective-permute-start(bf16[1,24,256]{2,1,0:T(8,128)(2,1)S(1)} %get-tuple-element.78), channel_id=1, source_target_pairs={{0,12},{4,8},{8,4},{12,0},{16,28},{20,24},{24,20},{28,16},{1,13},{... | collective-permute-start | bytes 36872 | tf_op jit(solution)/shard_map/ppermute | solution.py:95
  28.2 6.8 %collective-permute-start.3 = (bf16[1,24,256]{2,1,0:T(8,128)(2,1)S(1)}, bf16[1,24,256]{2,1,0:T(8,128)(2,1)S(1)}, u32[]{:S(2)}, u32[]{:S(2)}) collective-permute-start(bf16[1,24,256]{2,1,0:T(8,128)(2,1)S(1)} %get-tuple-element.77), channel_id=1, source_target_pairs={{0,16},{4,20},{8,24},{12,28},{16,0},{20,4},{24,8},{28,12},{1,17},{... | collective-permute-start | bytes 36872 | tf_op jit(solution)/shard_map/ppermute | solution.py:95
  30.8 7.6 %collective-permute-start.4 = (bf16[1,24,256]{2,1,0:T(8,128)(2,1)S(1)}, bf16[1,24,256]{2,1,0:T(8,128)(2,1)S(1)}, u32[]{:S(2)}, u32[]{:S(2)}) collective-permute-start(bf16[1,24,256]{2,1,0:T(8,128)(2,1)S(1)} %get-tuple-element.76), channel_id=1, source_target_pairs={{0,20},{4,16},{8,28},{12,24},{16,4},{20,0},{24,12},{28,8},{1,21},{... | collective-permute-start | bytes 36872 | tf_op jit(solution)/shard_map/ppermute | solution.py:95
  31.0 7.4 %collective-permute-start.5 = (bf16[1,24,256]{2,1,0:T(8,128)(2,1)S(1)}, bf16[1,24,256]{2,1,0:T(8,128)(2,1)S(1)}, u32[]{:S(2)}, u32[]{:S(2)}) collective-permute-start(bf16[1,24,256]{2,1,0:T(8,128)(2,1)S(1)} %get-tuple-element.75), channel_id=1, source_target_pairs={{0,24},{4,28},{8,16},{12,20},{16,8},{20,12},{24,0},{28,4},{1,25},{... | collective-permute-start | bytes 36872 | tf_op jit(solution)/shard_map/ppermute | solution.py:95
  34.7 4.9 %collective-permute-start.6 = (bf16[1,24,256]{2,1,0:T(8,128)(2,1)S(1)}, bf16[1,24,256]{2,1,0:T(8,128)(2,1)S(1)}, u32[]{:S(2)}, u32[]{:S(2)}) collective-permute-start(bf16[1,24,256]{2,1,0:T(8,128)(2,1)S(1)} %get-tuple-element.74), channel_id=1, source_target_pairs={{0,28},{4,24},{8,20},{12,16},{16,12},{20,8},{24,4},{28,0},{1,29},{... | collective-permute-start | bytes 36872 | tf_op jit(solution)/shard_map/ppermute | solution.py:95
  34.8 33.0 %collective-permute-start.7 = (bf16[24,1,128]{2,1,0:T(2,128)(2,1)S(1)}, bf16[24,1,128]{2,1,0:T(2,128)(2,1)S(1)}, u32[]{:S(2)}, u32[]{:S(2)}) collective-permute-start(bf16[24,1,128]{2,1,0:T(2,128)(2,1)S(1)} %get-tuple-element.72), channel_id=1, source_target_pairs={{0,4},{4,8},{8,12},{12,16},{16,20},{20,24},{24,28},{28,0},{1,5},{5... | collective-permute-start | bytes 18440 | tf_op jit(solution)/shard_map/ppermute | solution.py:18
  35.0 32.8 %collective-permute-start.8 = (bf16[24,1,128]{2,1,0:T(2,128)(2,1)S(1)}, bf16[24,1,128]{2,1,0:T(2,128)(2,1)S(1)}, u32[]{:S(2)}, u32[]{:S(2)}) collective-permute-start(bf16[24,1,128]{2,1,0:T(2,128)(2,1)S(1)} %get-tuple-element.73), channel_id=1, source_target_pairs={{4,0},{8,4},{12,8},{16,12},{20,16},{24,20},{28,24},{0,28},{5,1},{9... | collective-permute-start | bytes 18440 | tf_op jit(solution)/shard_map/ppermute | solution.py:21
  64.4 11.6 %all-to-all-start = ((f32[8,24,256]{2,1,0:T(8,128)}), f32[8,24,256]{2,1,0:T(8,128)S(1)}, u32[]{:S(2)}, u32[]{:S(2)}) async-start(f32[8,24,256]{2,1,0:T(8,128)} %bitcast.24), calls=%async_computation | async-start | bytes 393216 | tf_op jit(solution)/shard_map/all_to_all | solution.py:120
  67.8 33.2 %reduce-scatter.4.cloned.1.call-start = ((), (), s32[]{:S(2)}) async-start(), calls=%async_computation.2 | async-start | bytes 61440
  68.2 13.1 %collective-permute-start.10 = (bf16[24,66,1]{2,1,0:T(8,128)(2,1)S(1)}, bf16[24,66,1]{2,1,0:T(8,128)(2,1)S(1)}, u32[]{:S(2)}, u32[]{:S(2)}) collective-permute-start(bf16[24,66,1]{2,1,0:T(8,128)(2,1)S(1)} %get-tuple-element.71), channel_id=1, source_target_pairs={{1,0},{2,1},{3,2},{0,3},{5,4},{6,5},{7,6},{4,7},{9,8},{10,9},{11,1... | collective-permute-start | bytes 9512 | tf_op jit(solution)/shard_map/ppermute | solution.py:21
  69.8 21.7 %collective-permute-start.9 = (bf16[24,66,1]{2,1,0:T(8,128)(2,1)S(1)}, bf16[24,66,1]{2,1,0:T(8,128)(2,1)}, u32[]{:S(2)}, u32[]{:S(2)}) collective-permute-start(bf16[24,66,1]{2,1,0:T(8,128)(2,1)S(1)} %get-tuple-element.70), channel_id=1, source_target_pairs={{0,1},{1,2},{2,3},{3,0},{4,5},{5,6},{6,7},{7,4},{8,9},{9,10},{10,1... | collective-permute-start | bytes 9512 | tf_op jit(solution)/shard_map/ppermute | solution.py:18
  104.9 3.0 %copy-start.3 = (f32[24]{0:T(128)S(1)}, f32[24]{0:T(128)}, u32[]{:S(2)}) copy-start(f32[24]{0:T(128)} %param.15) | copy-start | bytes 292
  107.9 3.2 %copy-start.1 = (f32[24,64,128]{2,1,0:T(8,128)}, f32[24,64,128]{2,1,0:T(8,128)S(1)}, u32[]{:S(2)}) copy-start(f32[24,64,128]{2,1,0:T(8,128)S(1)} %copy.80) | copy-start | bytes 2359300
Sparse Core Ops, SparseCore 0:
  77.3 23.5 reduce-scatter.3
